TPU v7x, 256 devices: a whole 4x4x8 slice. The times are simulated.
256 devices in a mesh: row: 32 (over x_lo, z, core), col: 8 (over y, x_hi).
Axes of the slice: x: 4 (x_hi: 2, x_lo: 2; x = x_hi * 2 + x_lo), y: 4, z: 8, core: 2. Of those that a mesh axis runs over, the one named last changes fastest.
Arguments:
- trail_adjoint: float32 [32, 512, 8, 2048], P('row', None, 'col'), may hold values from -2.8 to 2.8, as said below
- panel_one: float32 [16384, 512], P(('row', 'col')), may hold values from -0.046875 to 0.046875
- panel_two: float32 [16384, 512], P(('row', 'col')), may hold values from -0.046875 to 0.046875
- upstream_one: float32 [16384, 512], P(('row', 'col')), may hold values from -6 to 6
- upstream_two: float32 [16384, 512], P(('row', 'col')), may hold values from -6 to 6
- pivot_one: float32 [512, 512], replicated, may hold values from -1 to 2, as said below
- pivot_two: float32 [512, 512], replicated, may hold values from -1 to 2, as said below
- link_block: float32 [512, 512], replicated, may hold values from -0.25 to 0.25
- pivot_adjoint: float32 [2, 512, 512], replicated, may hold values from -6 to 6
Outputs:
- strip_grad_one: float32 [16384, 512], P(('row', 'col'))
- strip_grad_two: float32 [16384, 512], P(('row', 'col'))
- block_grads: float32 [3, 512, 512], replicated
Inputs may be any that keep to these rules, and one draw needn't show every extreme that they name: trail_adjoint[a, c * 64 + s, c2, a2 * 64 + s2] equals trail_adjoint[a2, c2 * 64 + s2, c, a * 64 + s], so sbar is symmetric. `pivot_one`: lower triangular, diagonal entries between 1 and 2. `pivot_two`: lower triangular, diagonal entries between 1 and 2.
All inputs are finite; a program needn't handle non-finite values.
Results may differ from a plain program's by a relative error of at most 0.000062.
Values sent between devices are 32-bit elements; how exact they have to be, the bound alone decides.
No kernel may reach another device: no remote copies, remote signals or barrier semaphores. Data moves between devices by JAX's collectives and lax.ppermute only.
A program may use at most 128 MiB of HBM per device.

v0:
```python
import jax
import jax.numpy as jnp
from jax import lax
from jax.sharding import PartitionSpec as P


def exact_dot(left, right):
    return jnp.dot(left, right, precision=lax.Precision.HIGHEST, preferred_element_type=jnp.float32)


def cross_dot(left, right):
    return lax.dot_general(
        left,
        right,
        (((0,), (0,)), ((), ())),
        precision=lax.Precision.HIGHEST,
        preferred_element_type=jnp.float32,
    )


def lower_inverse(factor):
    identity = jnp.eye(factor.shape[0], dtype=jnp.float32)
    return jax.scipy.linalg.solve_triangular(factor, identity, lower=True)


def chol_grad(factor, cotangent, inverse):
    product = cross_dot(factor, jnp.tril(cotangent))
    halved = jnp.tril(product) - 0.5 * jnp.diag(jnp.diag(product))
    inner = cross_dot(inverse, exact_dot(halved, inverse))
    return 0.5 * (inner + inner.T)


def local(
    trail_adjoint,
    panel_one,
    panel_two,
    upstream_one,
    upstream_two,
    pivot_one,
    pivot_two,
    link_block,
    pivot_adjoint,
):
    width = panel_one.shape[1]
    stacked = jnp.concatenate([panel_one, panel_two], axis=1)
    matrix = trail_adjoint.reshape(trail_adjoint.shape[1], trail_adjoint.shape[3])
    summed = exact_dot(matrix, lax.all_gather(stacked, "row", axis=0, tiled=True))
    carried = lax.psum_scatter(2.0 * summed, "col", scatter_dimension=0, tiled=True)
    pressed_one = upstream_one - carried[:, :width]
    pressed_two = upstream_two - carried[:, width:]
    inverse_one = lower_inverse(pivot_one)
    inverse_two = lower_inverse(pivot_two)
    grad_two = exact_dot(pressed_two, inverse_two)
    cross_two, cross_link = lax.psum(
        (cross_dot(grad_two, panel_two), cross_dot(grad_two, panel_one)), ("row", "col")
    )
    grad_one = exact_dot(pressed_one - exact_dot(grad_two, link_block), inverse_one)
    cross_one = lax.psum(cross_dot(grad_one, panel_one), ("row", "col"))
    pivot_grad_two = chol_grad(pivot_two, pivot_adjoint[1] - cross_two, inverse_two)
    link_grad = -cross_link - 2.0 * exact_dot(pivot_grad_two, link_block)
    link_input = exact_dot(link_grad, inverse_one)
    pivot_grad_one = chol_grad(
        pivot_one, pivot_adjoint[0] - cross_dot(link_input, link_block) - cross_one, inverse_one
    )
    return (grad_one, grad_two, jnp.stack([pivot_grad_one, link_input, pivot_grad_two]))


def solution(mesh):
    return jax.shard_map(
        local,
        mesh=mesh,
        in_specs=(
            P("row", None, "col", None),
            P(("row", "col"), None),
            P(("row", "col"), None),
            P(("row", "col"), None),
            P(("row", "col"), None),
            P(),
            P(),
            P(),
            P(),
        ),
        out_specs=(P(("row", "col"), None), P(("row", "col"), None), P()),
        check_vma=False,
    )
```

profile of v0, /device:TPU:8, one launch (start us, length us, event | category | flops | bytes accessed | tf_op | source)
XLA Modules:
  0.0 531.6 jit_solution(8578837837325331191)
XLA Ops:
  7.2 1.8 pad_maximum_fusion.3
  9.1 1.8 copy.37
  10.9 1.3 fusion.16
  12.3 8.0 %while.4 = (s32[]{:T(128)}, f32[512,512]{1,0:T(8,128)S(1)}, s32[4,2]{0,1:T(2,128)S(1)}, f32[4,128,128]{2,1,0:T(8,128)S(1)}, s32[]{:T(128)}) while((s32[]{:T(128)}, f32[512,512]{1,0:T(8,128)S(1)}, s32[4,2]{0,1:T(2,128)S(1)}, f32[4,128,128]{2,1,0:T(8,128)S(1)}, s32[]{:T(128)}) %tuple.42), condition=%wide.while_cond, body=%wide.while_body.sunk | while | flops 2 | bytes 131189 | solution.py:23
  12.4 0.5 fusion.123
  12.9 1.4 bitcast_dynamic-update-slice_fusion.4
  14.4 0.5 fusion.123
  14.9 1.4 bitcast_dynamic-update-slice_fusion.4
  16.4 0.5 fusion.123
  16.9 1.4 bitcast_dynamic-update-slice_fusion.4
  18.4 0.5 fusion.123
  18.9 1.4 bitcast_dynamic-update-slice_fusion.4
  20.3 0.7 copy-done.22
  21.0 40.2 %custom-call.8 = f32[4,128,128]{1,2,0:T(8,128)S(1)} custom-call(f32[4,128,128]{2,1,0:T(8,128)} %copy-done.22), custom_call_target="InvertDiagBlocksLowerTriangular" | custom-call | tf_op jit(solution)/shard_map/jit(_solve_triangular)/triangular_solve | solution.py:23
  61.2 1.2 fusion.15
  62.4 24.2 %all-gather.2.cloned.1.call-done = f32[2048,1024]{1,0:T(8,128)} async-done(((f32[64,1024]{1,0:T(8,128)}), f32[2048,1024]{1,0:T(8,128)}) %all-gather.2.cloned.1.call-update) | async-done | bytes 8388624 | tf_op jit(solution)/shard_map/all_gather | solution.py:47
  86.6 32.1 %multiply_bitcast_fusion = f32[512,1024]{0,1:T(8,128)} fusion(f32[2048,1024]{1,0:T(8,128)} %all-gather.2.cloned.1.call-done, f32[1,512,1,2048]{3,2,1,0:T(1,128)} %param.11), kind=kOutput, calls=%fused_computation.10 | convolution fusion | flops 12885426176 | bytes 14680064 | tf_op jit(solution)/shard_map/dot_general | solution.py:8
  118.7 2.9 copy.44
  121.7 11.6 %while.5 = (s32[]{:T(128)}, f32[512,512]{1,0:T(8,128)}, s32[4,2]{0,1:T(2,128)S(1)}, f32[4,128,128]{2,1,0:T(8,128)S(1)}, s32[]{:T(128)}) while((s32[]{:T(128)}, f32[512,512]{1,0:T(8,128)}, s32[4,2]{0,1:T(2,128)S(1)}, f32[4,128,128]{2,1,0:T(8,128)S(1)}, s32[]{:T(128)}) %tuple.55), condition=%wide.while_cond.clone, body=%wide.while_body.clone.sunk | while | flops 2 | bytes 131189 | solution.py:23
  121.8 0.5 fusion.124
  122.3 2.3 bitcast_dynamic-update-slice_fusion.5
  124.7 0.5 fusion.124
  125.2 2.3 bitcast_dynamic-update-slice_fusion.5
  127.6 0.5 fusion.124
  128.1 2.3 bitcast_dynamic-update-slice_fusion.5
  130.5 0.5 fusion.124
  131.0 2.2 bitcast_dynamic-update-slice_fusion.5
  133.3 39.3 %custom-call.9 = f32[4,128,128]{1,2,0:T(8,128)S(1)} custom-call(f32[4,128,128]{2,1,0:T(8,128)S(1)} %get-tuple-element.19), custom_call_target="InvertDiagBlocksLowerTriangular" | custom-call | tf_op jit(solution)/shard_map/jit(_solve_triangular)/triangular_solve | solution.py:23
  172.7 0.4 fusion.58
  173.2 1.2 convolution_subtract_fusion.4
  174.4 0.4 fusion.72
  174.8 1.3 convolution_subtract_fusion.3
  176.6 1.6 convolution_subtract_fusion.6
  178.1 0.4 fusion.69
  179.0 1.2 convolution_subtract_fusion.2
  180.7 1.4 convolution_subtract_fusion.1
  182.1 1.3 fusion.66
  183.4 1.7 convolution_subtract_fusion.5
  185.1 1.3 fusion.65
  186.3 14.8 %reduce-scatter.4.cloned.1.call-done = f32[64,1024]{1,0:T(8,128)} async-done(((f32[512,1024]{1,0:T(8,128)}), f32[64,1024]{1,0:T(8,128)}) %reduce-scatter.4.cloned.1.call-update) | async-done | bytes 262160 | tf_op jit(solution)/shard_map/reduce_scatter | solution.py:48
  201.1 0.9 slice.56
  202.1 0.8 copy.47
  202.9 1.8 fusion.54
  204.7 3.0 fusion.92
  207.7 2.0 fusion.91
  209.7 1.7 convolution_subtract_fusion.7
  211.4 0.8 fusion.88
  212.2 2.1 fusion.93
  214.3 265.0 %all-reduce.3.cloned.1.call-done = (f32[512,512]{1,0:T(8,128)}, f32[512,512]{1,0:T(8,128)}, f32[512,512]{1,0:T(8,128)}) async-done(((f32[512,512]{1,0:T(8,128)}, f32[512,512]{1,0:T(8,128)}, f32[512,512]{1,0:T(8,128)}), (f32[512,512]{1,0:T(8,128)}, f32[512,512]{1,0:T(8,128)}, f32[512,512]{1,0:T(8,128)})) %all-reduce.3.cloned.1.call-update) | async-done | bytes 3145744 | tf_op jit(solution)/shard_map/psum | solution.py:54
  479.2 3.8 convolution_bitcast_fusion.1
  483.0 4.7 gather_fusion
  487.8 1.9 fusion.18
  489.6 1.9 fusion.62
  491.9 1.0 copy-done.1
  492.9 3.3 fusion.6
  496.3 1.9 fusion.87
  498.1 1.9 fusion.7
  500.1 2.9 convolution_bitcast_fusion
  503.0 8.7 %gather_fusion.1 = f32[512]{0:T(512)S(1)} fusion(f32[512,512]{1,0:T(8,128)} %convolution_bitcast_fusion, s32[512]{0:T(512)S(1)} %bitcast.110), kind=kCustom, calls=%fused_computation.1 | custom fusion | bytes 8192 | tf_op jit(solution)/shard_map/jit(_diag)/jit(diagonal)/cond/branch_0_fun/gather | solution.py:28
  511.7 3.4 fusion.21
  515.1 2.9 fusion.86
  518.0 2.5 copy.41
  520.5 2.4 fusion.9
  522.9 2.0 pad_maximum_fusion
  (70 shorter events, 2.6 us)
Async XLA Ops:
  7.2 202.5 %copy-start = (f32[512,512]{1,0:T(8,128)S(1)}, f32[512,512]{1,0:T(8,128)}, u32[]{:S(2)}) copy-start(f32[512,512]{1,0:T(8,128)} %param.18) | copy-start | bytes 3145732
  7.2 54.0 %copy-start.5 = (f32[512,512]{1,0:T(8,128)S(1)}, f32[512,512]{1,0:T(8,128)}, u32[]{:S(2)}) copy-start(f32[512,512]{1,0:T(8,128)} %param.16) | copy-start | bytes 3145732
  7.2 79.4 %all-gather.2.cloned.1.call-start = ((), (), s32[]{:S(2)}) async-start(), calls=%async_computation.1 | async-start | bytes 8650752 | tf_op jit(solution)/shard_map/all_gather | solution.py:47
  9.1 192.0 %reduce-scatter.4.cloned.1.call-start = ((), (), s32[]{:S(2)}) async-start(), calls=%async_computation.2 | async-start | bytes 2359296 | tf_op jit(solution)/shard_map/reduce_scatter | solution.py:48
  20.3 0.7 copy-start.22
  21.0 97.6 %copy-start.10 = (f32[512,512]{1,0:T(8,128)}, f32[512,512]{1,0:T(8,128)S(1)}, u32[]{:S(2)}) copy-start(f32[512,512]{1,0:T(8,128)S(1)} %get-tuple-element.153) | copy-start | bytes 3145732
  121.6 357.6 %all-reduce.3.cloned.1.call-start = ((), (), s32[]{:S(2)}) async-start(), calls=%async_computation.3 | async-start | bytes 6291456 | tf_op jit(solution)/shard_map/psum | solution.py:54
  172.6 7.6 %copy-start.20 = (f32[4,128,128]{1,2,0:T(8,128)}, f32[4,128,128]{1,2,0:T(8,128)S(1)}, u32[]{:S(2)}) copy-start(f32[4,128,128]{1,2,0:T(8,128)S(1)} %custom-call.9) | copy-start | bytes 786436
  178.6 24.3 %copy-start.18 = (f32[128,512]{1,0:T(8,128)}, f32[128,512]{1,0:T(8,128)S(1)}, u32[]{:S(2)}) copy-start(f32[128,512]{1,0:T(8,128)S(1)} %fusion.69) | copy-start | bytes 786436
  180.6 30.7 %copy-start.2 = (f32[128,512]{1,0:T(8,128)}, f32[128,512]{1,0:T(8,128)S(1)}, u32[]{:S(2)}) copy-start(f32[128,512]{1,0:T(8,128)S(1)} %fusion.68) | copy-start | bytes 786436
  182.1 25.6 %copy-start.16 = (f32[64,512]{1,0:T(8,128)S(1)}, f32[64,512]{1,0:T(8,128)}, u32[]{:S(2)}) copy-start(f32[64,512]{1,0:T(8,128)} %param.12) | copy-start | bytes 393220
  183.4 28.0 %copy-start.7 = (f32[128,512]{1,0:T(8,128)}, f32[128,512]{1,0:T(8,128)S(1)}, u32[]{:S(2)}) copy-start(f32[128,512]{1,0:T(8,128)S(1)} %fusion.66) | copy-start | bytes 786436
  186.3 25.1 %copy-start.11 = (f32[128,512]{1,0:T(8,128)}, f32[128,512]{1,0:T(8,128)S(1)}, u32[]{:S(2)}) copy-start(f32[128,512]{1,0:T(8,128)S(1)} %fusion.65) | copy-start | bytes 786436
  202.9 6.8 %copy-start.21 = (f32[64,1024]{1,0:T(8,128)S(1)}, f32[64,1024]{1,0:T(8,128)}, u32[]{:S(2)}) copy-start(f32[64,1024]{1,0:T(8,128)} %reduce-scatter.4.cloned.1.call-done) | copy-start | bytes 786436
  204.7 9.5 %copy-start.15 = (f32[64,512]{1,0:T(8,128)}, f32[64,512]{1,0:T(8,128)S(1)}, u32[]{:S(2)}) copy-start(f32[64,512]{1,0:T(8,128)S(1)} %fusion.54) | copy-start | bytes 393220
  212.1 267.1 %copy-start.23 = (f32[64,512]{1,0:T(8,128)}, f32[64,512]{1,0:T(8,128)S(1)}, u32[]{:S(2)}) copy-start(f32[64,512]{1,0:T(8,128)S(1)} %fusion.88) | copy-start | bytes 393220
  479.2 8.5 %copy-start.19 = (f32[128,512]{1,0:T(8,128)S(1)}, f32[128,512]{1,0:T(8,128)}, u32[]{:S(2)}) copy-start(f32[128,512]{1,0:T(8,128)} %copy-done.18) | copy-start | bytes 786436
  491.9 1.0 copy-start.1
  491.9 4.3 copy-start.3
  491.9 4.3 copy-start.8
  491.9 4.3 copy-start.12
  492.9 5.2 copy-start.14
  492.9 5.3 copy-start.17
  498.1 2.0 copy-start.6
  511.7 3.4 copy-start.4
  511.7 3.4 copy-start.9
  511.7 3.4 copy-start.13
Sparse Core Ops, SparseCore 0:
  10.5 76.0 all-gather.1
  121.7 79.3 reduce-scatter.3
  214.4 264.8 all-reduce.2
where the time goes:
time: 536 us; the launch traced here: 532 us
  waiting for transfers between devices  304 us (57%)
  other arithmetic  88.3 us (16%)
  matrix products  80.6 us (15%)
  local copies, waits for them, and re-layouts  43.9 us (8%)
  between operations  14.5 us (3%)
    psum x1, waiting for transfers between devices, local(): lax.psum((cross_dot(grad_two, panel_two), cross_dot(grad_two, panel_one))...  265 us
    another operation x5, other arithmetic, lower_inverse(): return jax.scipy.linalg.solve_triangular(factor, identity, lower=True)  82 us
    dot_general x8, matrix products, exact_dot(): jnp.dot(left, right, precision=lax.Precision.HIGHEST, preferred_element_t...  46.7 us
    all_gather x1, waiting for transfers between devices, local(): lax.all_gather(stacked, 'row', axis=0, tiled=True)  24.2 us
    dot_general x8, matrix products, cross_dot(): lax.dot_general(left, right, (((0,), (0,)), ((), ())), precision=lax.Prec...  20.5 us
    another operation x27, local copies, waits for them, and re-layouts, lower_inverse(): return jax.scipy.linalg.solve_triangular(factor, identity, lower=True)  19.4 us
    reduce_scatter x1, waiting for transfers between devices, local(): lax.psum_scatter(2.0 * summed, 'col', scatter_dimension=0, tiled=True)  14.8 us
    another operation x14, matrix products, lower_inverse(): return jax.scipy.linalg.solve_triangular(factor, identity, lower=True)  13.5 us
  transfers between devices with their start and end apart: 3, of which 3 were waited for; matrix products, arithmetic and copies ran while one was open for 22% of the time, Pallas kernels for 0%

commit v1 on v0

v1 whole, which is shorter than its diff:
```python
import jax
import jax.numpy as jnp
from jax import lax
from jax.experimental import pallas as pl
from jax.experimental.pallas import tpu as pltpu
from jax.sharding import Mesh, PartitionSpec as P

AXES = ("xl", "z", "core", "y", "xh")
ROW = ("xl", "z", "core")
COL = ("y", "xh")
PLANE = ("y", "xh", "xl")
HIGHEST = lax.Precision.HIGHEST
HIGH = lax.Precision.HIGH
SWAP = [(0, 1), (1, 0)]
W = 512
BASE = 16
VMEM_SPEC = pl.BlockSpec(memory_space=pltpu.VMEM)


def dot(left, right, precision=HIGHEST):
    return jnp.dot(left, right, precision=precision, preferred_element_type=jnp.float32)


def cross(left, right, precision=HIGHEST):
    return lax.dot_general(
        left, right, (((0,), (0,)), ((), ())), precision=precision, preferred_element_type=jnp.float32
    )


def iota(shape, dim):
    return lax.broadcasted_iota(jnp.int32, shape, dim)


def inverse_of(f_ref, v_ref):
    b = BASE
    lane = iota((b, W), 1)
    row = iota((b, W), 0)
    diag = jnp.zeros((b, W), jnp.float32)
    for k in range(W // b):
        diag = jnp.where(lane // b == k, f_ref[k * b : (k + 1) * b, :], diag)
    spread = (iota((128, 128), 0) // b == iota((128, 128), 1) // b).astype(jnp.float32)
    columns = []
    for t in range(W // 128):
        part = diag[:, t * 128 : (t + 1) * 128]
        inner = iota((b, 128), 1) % b
        stack = jnp.concatenate([jnp.where(inner == k, part, 0.0) for k in range(b)], axis=0)
        columns.append(dot(stack, spread))
    spread_f = jnp.concatenate(columns, axis=1)
    x = (lane % b == row).astype(jnp.float32)
    for k in range(b):
        f_k = spread_f[k * b : (k + 1) * b, :]
        x_k = x[k : k + 1, :] / f_k[k : k + 1, :]
        x = jnp.where(row == k, x_k, jnp.where(row > k, x - f_k * x_k, x))
    v_ref[...] = jnp.zeros((W, W), jnp.float32)
    r, c = iota((128, 128), 0), iota((128, 128), 1)
    for t in range(W // 128):
        s = slice(t * 128, (t + 1) * 128)
        part = jnp.concatenate([x[:, s]] * (128 // b), axis=0)
        v = jnp.where(r // b == c // b, part, 0.0)
        f = f_ref[s, s]
        size = b
        while size < 128:
            mask = (r // (2 * size) == c // (2 * size)) & (r // size > c // size)
            v = v - dot(v, dot(jnp.where(mask, f, 0.0), v))
            size *= 2
        v_ref[s, s] = v
    size = 128
    while size < W:
        for t in range(0, W, 2 * size):
            lo, hi = slice(t, t + size), slice(t + size, t + 2 * size)
            v_ref[hi, lo] = -dot(v_ref[hi, hi], dot(f_ref[hi, lo], v_ref[lo, lo]))
        size *= 2


def inverse_kernel(f1_ref, f2_ref, v1_ref, v2_ref):
    inverse_of(f1_ref, v1_ref)
    inverse_of(f2_ref, v2_ref)


def inverses(f1, f2):
    shape = jax.ShapeDtypeStruct((W, W), jnp.float32)
    return pl.pallas_call(
        inverse_kernel,
        out_shape=(shape, shape),
        in_specs=[VMEM_SPEC] * 2,
        out_specs=(VMEM_SPEC,) * 2,
        compiler_params=pltpu.CompilerParams(vmem_limit_bytes=32 << 20),
        cost_estimate=pl.CostEstimate(flops=10**10, bytes_accessed=4 << 20, transcendentals=0),
        name="inverses",
    )(f1, f2)


def split(x):
    hi = x.astype(jnp.bfloat16)
    return hi, (x - hi.astype(jnp.float32)).astype(jnp.bfloat16)


def dot_split(left, right, dims=(((1,), (0,)), ((), ()))):
    (a, b), (c, d) = left, right

    def one(x, y):
        return lax.dot_general(x, y, dims, preferred_element_type=jnp.float32)

    return one(a, c) + (one(b, c) + one(a, d))


def dot3(left, right):
    return dot_split(split(left), split(right))


def cross3(left, right):
    return dot_split(split(left), split(right), (((0,), (0,)), ((), ())))


CHUNKS, CHUNK_ROWS = 16, 136


def sums_kernel(core_ref, s_ref, g_ref, la_ref, u1_ref, u2_ref, l1_ref, l2_ref, p_ref, keep_ref, send_ref):
    step = pl.program_id(0)
    part = dot3(s_ref[...], g_ref[...])

    @pl.when(step == 0)
    def _():
        p_ref[...] = part

    @pl.when(step > 0)
    def _():
        p_ref[...] += part

    @pl.when(step == pl.num_programs(0) - 1)
    def _():
        p_ref[...] = -2.0 * p_ref[...]
        a22 = cross3(p_ref[:, W:], la_ref[:, W:]) + cross3(u2_ref[...], l2_ref[...])
        a21 = cross3(p_ref[:, W:], la_ref[:, :W]) + cross3(u2_ref[...], l1_ref[...])
        a11t = cross3(la_ref[:, :W], p_ref[:, :W]) + cross3(l1_ref[...], u1_ref[...])
        r, c = iota((W, W), 0), iota((W, W), 1)
        mixed = jnp.where(r >= c, a22, a11t)
        diagonal = jnp.sum(jnp.where(r == c, a11t, 0.0), axis=0, keepdims=True)

        def write(ref, x):
            for i in range(CHUNKS):
                for t in range(4):
                    ref[i, t * 32 : (t + 1) * 32, :] = x[i * 32 : (i + 1) * 32, t * 128 : (t + 1) * 128]
            ref[:, 128:, :] = jnp.zeros((CHUNKS, 8, 128), jnp.float32)

        def write_diagonal(ref):
            for t in range(4):
                ref[0, 128 + t : 129 + t, :] = diagonal[:, t * 128 : (t + 1) * 128]

        @pl.when(core_ref[0] == 0)
        def _():
            write(keep_ref, mixed)
            write_diagonal(keep_ref)
            write(send_ref, a21)

        @pl.when(core_ref[0] != 0)
        def _():
            write(keep_ref, a21)
            write(send_ref, mixed)
            write_diagonal(send_ref)


def sums(core, matrix, gathered, block_row, u1, u2, l1, l2):
    step = 512
    half = jax.ShapeDtypeStruct((CHUNKS, CHUNK_ROWS, 128), jnp.float32)
    return pl.pallas_call(
        sums_kernel,
        grid=(matrix.shape[1] // step,),
        out_shape=(jax.ShapeDtypeStruct((W, 2 * W), jnp.float32), half, half),
        in_specs=[
            pl.BlockSpec(memory_space=pltpu.SMEM),
            pl.BlockSpec((W, step), lambda k: (0, k)),
            pl.BlockSpec((step, 2 * W), lambda k: (k, 0)),
        ]
        + [VMEM_SPEC] * 5,
        out_specs=(VMEM_SPEC,) * 3,
        compiler_params=pltpu.CompilerParams(vmem_limit_bytes=48 << 20),
        cost_estimate=pl.CostEstimate(flops=10**10, bytes_accessed=20 << 20, transcendentals=0),
        name="sums",
    )(core, matrix, gathered, block_row, u1, u2, l1, l2)


def chol_grad(f, x, v, r, c):
    product = cross3(f, jnp.where(r >= c, x, 0.0))
    halved = jnp.where(r > c, product, jnp.where(r == c, 0.5 * product, 0.0))
    inner = cross3(v, dot3(halved, v))
    return 0.5 * (inner + inner.T)


def tail_kernel(
    core_ref, half_ref, other_ref, f1_ref, f2_ref, v1_ref, v2_ref, link_ref, adj_ref, out_ref, mixed_ref, a21_ref
):
    def read(ref, source):
        for i in range(CHUNKS):
            for t in range(4):
                ref[i * 32 : (i + 1) * 32, t * 128 : (t + 1) * 128] = source[i, t * 32 : (t + 1) * 32, :]

    first = core_ref[0] == 0

    @pl.when(first)
    def _():
        read(mixed_ref, half_ref)
        read(a21_ref, other_ref)

    @pl.when(jnp.logical_not(first))
    def _():
        read(mixed_ref, other_ref)
        read(a21_ref, half_ref)

    r, c = iota((W, W), 0), iota((W, W), 1)
    rows = jnp.where(first, half_ref[0, 128:, :], other_ref[0, 128:, :])
    diagonal = jnp.concatenate([rows[t : t + 1, :] for t in range(4)], axis=1)
    mixed = mixed_ref[...]
    a22 = jnp.where(r >= c, mixed, 0.0)
    a11 = jnp.where(r > c, mixed.T, jnp.where(r == c, diagonal, 0.0))
    link, v1, v2 = link_ref[...], v1_ref[...], v2_ref[...]
    grad_two = chol_grad(f2_ref[...], adj_ref[1] - cross3(v2, a22), v2, r, c)
    out_ref[2] = grad_two
    cross_link = cross3(v2, a21_ref[...])
    cross_one = cross3(v1, a11 - cross3(link, cross_link))
    link_input = dot3(-cross_link - 2.0 * dot3(grad_two, link), v1)
    out_ref[1] = link_input
    out_ref[0] = chol_grad(f1_ref[...], adj_ref[0] - cross3(link_input, link) - cross_one, v1, r, c)


def tail(core, *operands):
    return pl.pallas_call(
        tail_kernel,
        out_shape=jax.ShapeDtypeStruct((3, W, W), jnp.float32),
        in_specs=[pl.BlockSpec(memory_space=pltpu.SMEM)] + [VMEM_SPEC] * 8,
        out_specs=VMEM_SPEC,
        scratch_shapes=[pltpu.VMEM((W, W), jnp.float32)] * 2,
        compiler_params=pltpu.CompilerParams(vmem_limit_bytes=48 << 20),
        cost_estimate=pl.CostEstimate(flops=10**10, bytes_accessed=14 << 20, transcendentals=0),
        name="tail",
    )(core, *operands)


def reduce_all(keep, send):
    half = keep + lax.ppermute(send, "core", SWAP)
    share = jnp.sum(lax.all_to_all(half, PLANE, 0, 0, tiled=True), axis=0)
    for d in (1, 2, 4):
        share = share + lax.ppermute(share, "z", [(i, i ^ d) for i in range(8)])
    half = lax.all_to_all(jnp.broadcast_to(share, half.shape), PLANE, 0, 0, tiled=True)
    return half, lax.ppermute(half, "core", SWAP)


def local(trail, l1, l2, u1, u2, f1, f2, link, adjoint):
    core = lax.axis_index("core").reshape(1)
    own = jnp.concatenate([l1, l2], axis=1)
    gathered = lax.all_gather(own, ROW, axis=0, tiled=True)
    block_row = lax.all_to_all(jnp.tile(own, (8, 1)), COL, 0, 0, tiled=True)
    matrix = trail.reshape(W, 2048)
    v1, v2 = inverses(f1, f2)
    gathered, block_row, matrix, v1, v2 = lax.optimization_barrier((gathered, block_row, matrix, v1, v2))
    product, keep, send = sums(core, matrix, gathered, block_row, u1, u2, l1, l2)
    half, other = reduce_all(keep, send)
    product, half, other = lax.optimization_barrier((product, half, other))
    mine = lax.all_to_all(product, COL, 0, 0, tiled=True)
    grads = tail(core, half, other, f1, f2, v1, v2, link, adjoint)
    pressed = jnp.sum(mine.reshape(8, 64, 2 * W), axis=0)
    grad_two = dot(u2 + pressed[:, W:], v2)
    grad_one = dot(u1 + pressed[:, :W] - dot(grad_two, link), v1)
    return grad_one, grad_two, grads


def solution(mesh):
    fine = Mesh(mesh.devices.reshape(2, 8, 2, 4, 2), AXES)
    strip = P(ROW + COL, None)
    return jax.shard_map(
        local,
        mesh=fine,
        in_specs=(P(ROW, None, COL, None), strip, strip, strip, strip, P(), P(), P(), P()),
        out_specs=(strip, strip, P()),
        check_vma=False,
    )
```

time: 536 us -> 229 us (0.43)
  waiting for transfers between devices: 304 us -> 85.1 us
  other arithmetic: 88.3 us -> 2.65 us
  matrix products: 80.6 us -> 4.78 us
  Pallas kernels: 0 us -> 43.6 us
  blocking collectives: 0 us -> 41.8 us
  local copies, waits for them, and re-layouts: 43.9 us -> 14.9 us
  starting transfers between devices: 0.12 us -> 20.3 us
    psum x1 -> x0, waiting for transfers between devices: 265 us -> none  [local(): lax.psum((cross_dot(grad_two, panel_two), cross_dot(grad_two, panel_one))...]
    another operation x7 -> x0, other arithmetic: 86.3 us -> none  [the longest x5 82 us: lower_inverse(): return jax.scipy.linalg.solve_triangular(factor, identity, lower=True)]
    dot_general x16 -> x3, matrix products: 67.2 us -> 4.78 us  [dot(): jnp.dot(left, right, precision=precision, preferred_element_type=jnp.floa...]
    pallas_call x0 -> x3, Pallas kernels: none -> 43.6 us  [the longest x1 16.3 us: sums(): pl.pallas_call(sums_kernel, grid=(matrix.shape[1] // step,), out_shape=(j...]
    all_to_all x0 -> x2, blocking collectives: none -> 41.8 us  [the longest x1 24.9 us: reduce_all(): share = jnp.sum(lax.all_to_all(half, PLANE, 0, 0, tiled=True), axis=0)]
    all_to_all x0 -> x2, waiting for transfers between devices: none -> 36.1 us  [the longest x1 27.1 us: local(): block_row = lax.all_to_all(jnp.tile(own, (8, 1)), COL, 0, 0, tiled=True)]
    ppermute x0 -> x5, waiting for transfers between devices: none -> 17.2 us  [the longest x3 12 us: reduce_all(): share = share + lax.ppermute(share, 'z', [(i, i ^ d) for i in range(8)])]
    another operation x27 -> x1, local copies, waits for them, and re-layouts: 19.4 us -> 2.52 us  [local(): block_row = lax.all_to_all(jnp.tile(own, (8, 1)), COL, 0, 0, tiled=True)]
  transfers between devices with their start and end apart: 3 -> 8, of which waited for: 3 -> 8; matrix products, arithmetic and copies ran while one was open for 22% -> 4% of each run, Pallas kernels for 0% -> 12%
where the time goes in v1:
time: 229 us; the launch traced here: 227 us
  waiting for transfers between devices  85.1 us (37%)
  Pallas kernels  43.6 us (19%)
  blocking collectives  41.8 us (18%)
  starting transfers between devices  20.3 us (9%)
  local copies, waits for them, and re-layouts  14.9 us (7%)
  between operations  14.1 us (6%)
  matrix products  4.78 us (2%)
  other arithmetic  2.65 us (1%)
    all_gather x1, waiting for transfers between devices, local(): gathered = lax.all_gather(own, ROW, axis=0, tiled=True)  31.8 us
    all_to_all x1, waiting for transfers between devices, local(): block_row = lax.all_to_all(jnp.tile(own, (8, 1)), COL, 0, 0, tiled=True)  27.1 us
    all_to_all x1, blocking collectives, reduce_all(): share = jnp.sum(lax.all_to_all(half, PLANE, 0, 0, tiled=True), axis=0)  24.9 us
    all_to_all x1, blocking collectives, reduce_all(): lax.all_to_all(jnp.broadcast_to(share, half.shape), PLANE, 0, 0, tiled=True)  16.9 us
    pallas_call x1, Pallas kernels, sums(): pl.pallas_call(sums_kernel, grid=(matrix.shape[1] // step,), out_shape=(j...  16.3 us
    pallas_call x1, Pallas kernels, tail(): pl.pallas_call(tail_kernel, out_shape=jax.ShapeDtypeStruct((3, W, W), jnp...  15.9 us
    ppermute x3, waiting for transfers between devices, reduce_all(): share = share + lax.ppermute(share, 'z', [(i, i ^ d) for i in range(8)])  12 us
    unnamed x28, local copies, waits for them, and re-layouts  11.4 us
  transfers between devices with their start and end apart: 8, of which 8 were waited for; matrix products, arithmetic and copies ran while one was open for 4% of the time, Pallas kernels for 12%

profile of v1, /device:TPU:8, one launch (start us, length us, event | category | flops | bytes accessed | tf_op | source)
XLA Modules:
  0.0 227.2 jit_solution(14906767143291347231)
XLA Ops:
  7.2 0.0 all-gather.2.cloned.1.call-start
  7.2 0.9 constant_dynamic-update-slice_fusion.1
  8.1 0.9 constant_dynamic-update-slice_fusion
  9.0 0.0 copy-start.9
  9.1 0.7 copy-done.9
  9.8 0.0 all-gather.2.cloned.1.call-update
  9.8 2.5 %tile.2 = f32[8,64,1024]{2,1,0:T(8,128)} broadcast(f32[64,1024]{1,0:T(8,128)} %copy-done.9), dimensions={1,2} | broadcast | bytes 2359296 | tf_op jit(solution)/shard_map/tile | solution.py:252
  12.3 7.4 %all-to-all-start = ((f32[8,64,1024]{2,1,0:T(8,128)}), f32[8,64,1024]{2,1,0:T(8,128)}, u32[]{:S(2)}, u32[]{:S(2)}) async-start(f32[8,64,1024]{2,1,0:T(8,128)} %tile.2), calls=%async_computation | async-start | bytes 4194304 | tf_op jit(solution)/shard_map/all_to_all | solution.py:252
  19.7 0.0 copy-start.5
  19.7 0.0 copy-start.7
  19.7 6.3 %copy.14 = f32[1,512,1,2048]{3,1,2,0:T(8,128)} copy(f32[1,512,1,2048]{3,2,1,0:T(1,128)} %param.9) | data formatting | bytes 8388608
  26.0 0.0 copy-done.5
  26.0 0.0 copy-done.7
  26.0 0.0 copy-start.1
  26.0 0.0 copy-start.2
  26.0 0.0 copy-start.3
  26.0 0.0 copy-start.4
  26.0 11.4 %inverses.1 = (f32[512,512]{1,0:T(8,128)S(1)}, f32[512,512]{1,0:T(8,128)S(1)}) custom-call(f32[512,512]{1,0:T(8,128)S(1)} %copy-done.5, f32[512,512]{1,0:T(8,128)S(1)} %copy-done.7), custom_call_target="tpu_custom_call" | custom-call | flops 10000000000 | bytes 4194304 | tf_op jit(solution)/shard_map/inverses/pallas_call | solution.py:82
  37.4 27.1 %all-to-all-done = f32[8,64,1024]{2,1,0:T(8,128)} async-done(((f32[8,64,1024]{2,1,0:T(8,128)}), f32[8,64,1024]{2,1,0:T(8,128)}, u32[]{:S(2)}, u32[]{:S(2)}) %all-to-all-start) | async-done | bytes 2097184 | tf_op jit(solution)/shard_map/all_to_all | solution.py:252
  64.5 31.8 %all-gather.2.cloned.1.call-done.g_ref = f32[2048,1024]{1,0:T(8,128)} async-done(((f32[64,1024]{1,0:T(8,128)}), f32[2048,1024]{1,0:T(8,128)}) %all-gather.2.cloned.1.call-update) | async-done | bytes 8388624 | tf_op jit(solution)/shard_map/all_gather | solution.py:251
  96.2 0.0 copy-done.1
  96.2 0.0 copy-done.2
  96.3 0.0 copy-done.3
  96.3 0.0 copy-done.4
  96.3 16.3 %sums.1 = (f32[512,1024]{1,0:T(8,128)}, f32[16,136,128]{2,1,0:T(8,128)S(1)}, f32[16,136,128]{2,1,0:T(8,128)S(1)}) custom-call(s32[1]{0:T(128)} %bitcast.core_ref, f32[512,2048]{1,0:T(8,128)} %bitcast.11, f32[2048,1024]{1,0:T(8,128)} %all-gather.2.cloned.1.call-done.g_ref, f32[512,1024]{1,0:T(8,128)} %bitcast.1.la_ref, f32[64,512]{1,0:T(8,128)S(1)} %copy-done.1, ...), custom_call_target="tpu_custom_call" | custom-call | flops 10000000000 | bytes 20971520 | tf_op jit(solution)/shard_map/sums/pallas_call | solution.py:166
  112.6 0.3 collective-permute-start
  112.9 2.5 %collective-permute-done = f32[16,136,128]{2,1,0:T(8,128)S(1)} collective-permute-done((f32[16,136,128]{2,1,0:T(8,128)S(1)}, f32[16,136,128]{2,1,0:T(8,128)S(1)}, u32[]{:S(2)}, u32[]{:S(2)}) %collective-permute-start) | collective-permute-done | bytes 1114144 | tf_op jit(solution)/shard_map/ppermute | solution.py:240
  115.3 0.1 add.18
  115.5 24.9 %all_to_all.28 = f32[16,136,128]{2,1,0:T(8,128)S(1)} all-to-all(f32[16,136,128]{2,1,0:T(8,128)S(1)} %add.18), channel_id=1, replica_groups=mesh['xl'=2,'z'=8,'core'=2,'y'=4,'xh'=2] {'y','xh','xl'}, dimensions={0} | all-to-all | bytes 2228224 | tf_op jit(solution)/shard_map/all_to_all | solution.py:241
  140.3 0.1 reduce_sum.18
  140.4 0.6 collective-permute-start.1
  141.0 3.8 %collective-permute-done.1 = f32[136,128]{1,0:T(8,128)S(1)} collective-permute-done((f32[136,128]{1,0:T(8,128)S(1)}, f32[136,128]{1,0:T(8,128)S(1)}, u32[]{:S(2)}, u32[]{:S(2)}) %collective-permute-start.1) | collective-permute-done | bytes 69664 | tf_op jit(solution)/shard_map/ppermute | solution.py:243
  144.8 2.4 %collective-permute-start.2 = (f32[136,128]{1,0:T(8,128)S(1)}, f32[136,128]{1,0:T(8,128)S(1)}, u32[]{:S(2)}, u32[]{:S(2)}) collective-permute-start(f32[136,128]{1,0:T(8,128)S(1)} %add.19), channel_id=1, source_target_pairs={{0,32},{16,48},{32,0},{48,16},{64,96},{80,112},{96,64},{112,80},{1... | collective-permute-start | bytes 208904 | tf_op jit(solution)/shard_map/ppermute | solution.py:243
  147.2 3.6 %collective-permute-done.2 = f32[136,128]{1,0:T(8,128)S(1)} collective-permute-done((f32[136,128]{1,0:T(8,128)S(1)}, f32[136,128]{1,0:T(8,128)S(1)}, u32[]{:S(2)}, u32[]{:S(2)}) %collective-permute-start.2) | collective-permute-done | bytes 69664 | tf_op jit(solution)/shard_map/ppermute | solution.py:243
  150.8 3.7 %collective-permute-start.3 = (f32[136,128]{1,0:T(8,128)S(1)}, f32[136,128]{1,0:T(8,128)S(1)}, u32[]{:S(2)}, u32[]{:S(2)}) collective-permute-start(f32[136,128]{1,0:T(8,128)S(1)} %add.20), channel_id=1, source_target_pairs={{0,64},{16,80},{32,96},{48,112},{64,0},{80,16},{96,32},{112,48},{1... | collective-permute-start | bytes 208904 | tf_op jit(solution)/shard_map/ppermute | solution.py:243
  154.6 4.6 %collective-permute-done.3 = f32[136,128]{1,0:T(8,128)S(1)} collective-permute-done((f32[136,128]{1,0:T(8,128)S(1)}, f32[136,128]{1,0:T(8,128)S(1)}, u32[]{:S(2)}, u32[]{:S(2)}) %collective-permute-start.3) | collective-permute-done | bytes 69664 | tf_op jit(solution)/shard_map/ppermute | solution.py:243
  159.2 0.1 broadcast_in_dim.3
  159.2 16.9 %all_to_all.29.half_ref = f32[16,136,128]{2,1,0:T(8,128)S(1)} all-to-all(f32[16,136,128]{2,1,0:T(8,128)S(1)} %broadcast_in_dim.3), channel_id=1, replica_groups=mesh['xl'=2,'z'=8,'core'=2,'y'=4,'xh'=2] {'y','xh','xl'}, dimensions={0} | all-to-all | bytes 2228224 | tf_op jit(solution)/shard_map/all_to_all | solution.py:244
  176.1 0.0 copy-start.10
  176.1 0.0 collective-permute-start.4
  176.2 2.8 %collective-permute-done.4.other_ref = f32[16,136,128]{2,1,0:T(8,128)S(1)} collective-permute-done((f32[16,136,128]{2,1,0:T(8,128)S(1)}, f32[16,136,128]{2,1,0:T(8,128)S(1)}, u32[]{:S(2)}, u32[]{:S(2)}) %collective-permute-start.4) | collective-permute-done | bytes 1114144 | tf_op jit(solution)/shard_map/ppermute | solution.py:245
  178.9 0.0 copy-start.12
  178.9 0.0 copy-done.10
  178.9 1.0 copy-done.12
  179.9 0.0 copy-start
  179.9 5.9 %all-to-all-start.3 = ((f32[8,64,1024]{2,1,0:T(8,128)}), f32[8,64,1024]{2,1,0:T(8,128)}, u32[]{:S(2)}, u32[]{:S(2)}) async-start(f32[8,64,1024]{2,1,0:T(8,128)} %bitcast.2), calls=%async_computation.3 | async-start | bytes 4194304 | tf_op jit(solution)/shard_map/all_to_all | solution.py:259
  185.7 0.0 copy-done
  185.8 0.0 copy-start.6
  185.8 1.2 copy-done.6
  187.0 0.0 copy-start.8
  187.0 1.2 copy-done.8
  188.2 15.9 %tail.1 = f32[3,512,512]{2,1,0:T(8,128)} custom-call(s32[1]{0:T(128)} %bitcast.core_ref, f32[16,136,128]{2,1,0:T(8,128)} %copy-done.10, f32[16,136,128]{2,1,0:T(8,128)} %copy-done.12, f32[512,512]{1,0:T(8,128)S(1)} %copy-done.6, f32[512,512]{1,0:T(8,128)S(1)} %copy-done.8, f32[512,512]{1,0:T(8,128)S(1)} %get-tuple-element.26.v1_ref, ...), custom_call_target="tpu_custom_call" | custom-call | flops 10000000000 | bytes 14680064 | tf_op jit(solution)/shard_map/tail/pallas_call | solution.py:227
  204.1 9.1 %all-to-all-done.3 = f32[8,64,1024]{2,1,0:T(8,128)} async-done(((f32[8,64,1024]{2,1,0:T(8,128)}), f32[8,64,1024]{2,1,0:T(8,128)}, u32[]{:S(2)}, u32[]{:S(2)}) %all-to-all-start.3) | async-done | bytes 2097184 | tf_op jit(solution)/shard_map/all_to_all | solution.py:259
  213.2 2.4 %reduce_sum.19 = f32[64,1024]{1,0:T(8,128)} reduce(f32[8,64,1024]{2,1,0:T(8,128)} %all-to-all-done.3, f32[]{:T(128)} %constant.7.clone.1), dimensions={0}, to_apply=%region_1.0 | reduce | flops 458752 | bytes 2359300 | tf_op jit(solution)/shard_map/reduce_sum | solution.py:261
  215.6 1.7 fusion
  217.3 0.0 copy-start.11
  217.3 1.7 convolution_subtract_fusion
  219.0 1.4 fusion.1
  220.4 0.0 copy-done.11
  (3 shorter events, 0.0 us)
Async XLA Ops:
  7.2 89.1 %all-gather.2.cloned.1.call-start = ((), (), s32[]{:S(2)}) async-start(), calls=%async_computation.4 | async-start | bytes 8650752 | tf_op jit(solution)/shard_map/all_gather | solution.py:251
  9.0 0.7 copy-start.9
  12.3 52.1 %all-to-all-start = ((f32[8,64,1024]{2,1,0:T(8,128)}), f32[8,64,1024]{2,1,0:T(8,128)}, u32[]{:S(2)}, u32[]{:S(2)}) async-start(f32[8,64,1024]{2,1,0:T(8,128)} %tile.2), calls=%async_computation | async-start | bytes 4194304 | tf_op jit(solution)/shard_map/all_to_all | solution.py:252
  19.7 6.3 %copy-start.5 = (f32[512,512]{1,0:T(8,128)S(1)}, f32[512,512]{1,0:T(8,128)}, u32[]{:S(2)}) copy-start(f32[512,512]{1,0:T(8,128)} %f1_ref.3) | copy-start | bytes 3145732
  19.7 6.3 %copy-start.7 = (f32[512,512]{1,0:T(8,128)S(1)}, f32[512,512]{1,0:T(8,128)}, u32[]{:S(2)}) copy-start(f32[512,512]{1,0:T(8,128)} %f2_ref.3) | copy-start | bytes 3145732
  26.0 70.3 %copy-start.1 = (f32[64,512]{1,0:T(8,128)S(1)}, f32[64,512]{1,0:T(8,128)}, u32[]{:S(2)}) copy-start(f32[64,512]{1,0:T(8,128)} %u1_ref.1) | copy-start | bytes 393220
  26.0 70.3 %copy-start.2 = (f32[64,512]{1,0:T(8,128)S(1)}, f32[64,512]{1,0:T(8,128)}, u32[]{:S(2)}) copy-start(f32[64,512]{1,0:T(8,128)} %l1_ref.1) | copy-start | bytes 393220
  26.0 70.3 %copy-start.3 = (f32[64,512]{1,0:T(8,128)S(1)}, f32[64,512]{1,0:T(8,128)}, u32[]{:S(2)}) copy-start(f32[64,512]{1,0:T(8,128)} %l2_ref.1) | copy-start | bytes 393220
  26.0 70.3 %copy-start.4 = (f32[64,512]{1,0:T(8,128)S(1)}, f32[64,512]{1,0:T(8,128)}, u32[]{:S(2)}) copy-start(f32[64,512]{1,0:T(8,128)} %u2_ref.1) | copy-start | bytes 393220
  112.6 2.8 %collective-permute-start = (f32[16,136,128]{2,1,0:T(8,128)S(1)}, f32[16,136,128]{2,1,0:T(8,128)S(1)}, u32[]{:S(2)}, u32[]{:S(2)}) collective-permute-start(f32[16,136,128]{2,1,0:T(8,128)S(1)} %get-tuple-element.23), channel_id=1, source_target_pairs={{0,8},{8,0},{1,9},{9,1},{2,10},{10,2},{3,11},{11,3},{4,12},{12,4},... | collective-permute-start | bytes 3342344 | tf_op jit(solution)/shard_map/ppermute | solution.py:240
  140.4 4.4 %collective-permute-start.1 = (f32[136,128]{1,0:T(8,128)S(1)}, f32[136,128]{1,0:T(8,128)S(1)}, u32[]{:S(2)}, u32[]{:S(2)}) collective-permute-start(f32[136,128]{1,0:T(8,128)S(1)} %reduce_sum.18), channel_id=1, source_target_pairs={{0,16},{16,0},{32,48},{48,32},{64,80},{80,64},{96,112},{112,96},{1... | collective-permute-start | bytes 208904 | tf_op jit(solution)/shard_map/ppermute | solution.py:243
  144.8 6.0 %collective-permute-start.2 = (f32[136,128]{1,0:T(8,128)S(1)}, f32[136,128]{1,0:T(8,128)S(1)}, u32[]{:S(2)}, u32[]{:S(2)}) collective-permute-start(f32[136,128]{1,0:T(8,128)S(1)} %add.19), channel_id=1, source_target_pairs={{0,32},{16,48},{32,0},{48,16},{64,96},{80,112},{96,64},{112,80},{1... | collective-permute-start | bytes 208904 | tf_op jit(solution)/shard_map/ppermute | solution.py:243
  150.8 8.3 %collective-permute-start.3 = (f32[136,128]{1,0:T(8,128)S(1)}, f32[136,128]{1,0:T(8,128)S(1)}, u32[]{:S(2)}, u32[]{:S(2)}) collective-permute-start(f32[136,128]{1,0:T(8,128)S(1)} %add.20), channel_id=1, source_target_pairs={{0,64},{16,80},{32,96},{48,112},{64,0},{80,16},{96,32},{112,48},{1... | collective-permute-start | bytes 208904 | tf_op jit(solution)/shard_map/ppermute | solution.py:243
  176.1 2.8 %copy-start.10 = (f32[16,136,128]{2,1,0:T(8,128)}, f32[16,136,128]{2,1,0:T(8,128)S(1)}, u32[]{:S(2)}) copy-start(f32[16,136,128]{2,1,0:T(8,128)S(1)} %all_to_all.29.half_ref) | copy-start | bytes 3342340
  176.1 2.8 %collective-permute-start.4 = (f32[16,136,128]{2,1,0:T(8,128)S(1)}, f32[16,136,128]{2,1,0:T(8,128)S(1)}, u32[]{:S(2)}, u32[]{:S(2)}) collective-permute-start(f32[16,136,128]{2,1,0:T(8,128)S(1)} %all_to_all.29.half_ref), channel_id=1, source_target_pairs={{0,8},{8,0},{1,9},{9,1},{2,10},{10,2},{3,11},{11,3},{4,12},{12,4},... | collective-permute-start | bytes 3342344 | tf_op jit(solution)/shard_map/ppermute | solution.py:245
  178.9 1.0 copy-start.12
  179.9 5.9 %copy-start = (f32[512,512]{1,0:T(8,128)S(1)}, f32[512,512]{1,0:T(8,128)}, u32[]{:S(2)}) copy-start(f32[512,512]{1,0:T(8,128)} %link_ref.1) | copy-start | bytes 3145732
  179.9 33.3 %all-to-all-start.3 = ((f32[8,64,1024]{2,1,0:T(8,128)}), f32[8,64,1024]{2,1,0:T(8,128)}, u32[]{:S(2)}, u32[]{:S(2)}) async-start(f32[8,64,1024]{2,1,0:T(8,128)} %bitcast.2), calls=%async_computation.3 | async-start | bytes 4194304 | tf_op jit(solution)/shard_map/all_to_all | solution.py:259
  185.8 1.2 copy-start.6
  187.0 1.2 copy-start.8
  217.3 3.1 %copy-start.11 = (f32[64,512]{1,0:T(8,128)}, f32[64,512]{1,0:T(8,128)S(1)}, u32[]{:S(2)}) copy-start(f32[64,512]{1,0:T(8,128)S(1)} %fusion) | copy-start | bytes 393220
Sparse Core Ops, SparseCore 0:
  9.9 86.2 all-gather.1
